TPU v7x, 256 devices: a whole 4x4x8 slice. The times are simulated.
256 devices in a mesh: depth: 32 (over z, x), tile: 8 (over y, core).
Axes of the slice: x: 4, y: 4, z: 8, core: 2. Of those that a mesh axis runs over, the one named last changes fastest.
Arguments:
- tidal: float32 [32, 3, 131072], P('depth', None, 'tile'), may hold values from -1.5 to 1.5
- plane_weight: float32 [32], P('depth'), may hold values from 0.2 to 1
- plane_step: float32 [32], P('depth'), may hold values from 0.2 to 0.6
- ray_angle: float32 [131072], P('tile'), may hold values from -3.140625 to 3.140625
- dest_tile: int32 [32, 1024, 1], P('depth', 'tile'), may hold values from 0 to 7; in each aligned block of 128 rows (0 to 127, 128 to 255, ..., all dimensions but the last counted through in order) at most 32 rows name the same one
- dest_segment: int32 [32, 1024], P('depth', 'tile'), may hold values from 0 to 255
- interp: bfloat16 [32, 1024, 128, 128], P('depth', 'tile'), may hold values from -0.5 to 0.5
Outputs:
- potential_adjoint: float32 [32, 16, 16384], P('depth', 'tile')
Inputs may be any that keep to these rules, and one draw needn't show every extreme that they name: `dest_tile`: in each plane, the 128 blocks of one strip name no strip more than 32 times, a bound that some block reaches.
All inputs are finite; a program needn't handle non-finite values.
Results may differ from a plain program's by a relative error of at most 0.003.
Values sent between devices are 32-bit elements; how exact they have to be, the bound alone decides.
A program may use at most 64 MiB of HBM per device.

v0:
```python
import jax
import jax.numpy as jnp
from jax import lax
from jax.sharding import PartitionSpec as P

ROWS = 2
COLS = 16384


def from_behind(value, axis, steps):
    count = lax.axis_size(axis)
    leading, last = (max(0, -steps), min(count, count - steps))
    return lax.ppermute(value, axis, [(source, source + steps) for source in range(leading, last)])


def padded_2(shard, sides, width):
    for axis, dim in sides:
        count, length = (lax.axis_size(axis), shard.shape[dim])
        up = [(i, (i + 1) % count) for i in range(count - 1)]
        down = [(j, i) for i, j in up]
        last = lax.slice_in_dim(shard, length - width, length, axis=dim)
        leading = lax.slice_in_dim(shard, 0, width, axis=dim)
        before = lax.ppermute(last, axis, up)
        after = lax.ppermute(leading, axis, down)
        shard = jnp.concatenate([before, shard, after], axis=dim)
    return shard


def column_part(field):
    padded = jnp.pad(field, ((0, 0), (0, 0), (1, 1)))
    return 0.5 * (padded[:, :, :-2] - padded[:, :, 2:])


def smooth_cols(field):
    padded = jnp.pad(field, ((0, 0), (0, 0), (1, 1)))
    return 0.25 * padded[:, :, :-2] + 0.5 * field + 0.25 * padded[:, :, 2:]


def per_device(tidal, plane_weight, plane_step, ray_angle, dest_tile, dest_segment, interp):
    planes_here = tidal.shape[0]
    n_tile = lax.axis_size("tile")
    n_depth = lax.axis_size("depth")
    blocks_here = interp.shape[1]
    width = interp.shape[2]
    slots = 2 * blocks_here // n_tile
    segments = ROWS * COLS // width
    jxx = tidal[:, 0]
    jxy = tidal[:, 1]
    jyy = tidal[:, 2]
    local_terms = jnp.stack(
        [
            -jnp.sum(plane_weight[:, None] * (jxx - jyy) * 0.5, axis=0),
            -jnp.sum(plane_weight[:, None] * jxy, axis=0),
        ]
    )
    shear = lax.psum(local_terms, "depth")
    cross = -shear[0] * jnp.sin(2.0 * ray_angle) + shear[1] * jnp.cos(2.0 * ray_angle)
    seed_state = jnp.stack(
        [
            cross * jnp.cos(ray_angle),
            cross * jnp.sin(ray_angle),
            jnp.zeros_like(cross),
            jnp.zeros_like(cross),
        ]
    )

    def sweep(top):
        xb_one, xb_two, tb_one, tb_two = (top[0], top[1], top[2], top[3])
        step_len = plane_step[0]
        tp_one = tb_one + step_len * xb_one
        tp_two = tb_two + step_len * xb_two
        adjoints = [jnp.stack([-tp_one, -tp_two])]
        new_one = xb_one - (jxx[0] * tp_one + jxy[0] * tp_two)
        new_two = xb_two - (jxy[0] * tp_one + jyy[0] * tp_two)
        return (jnp.stack([new_one, new_two, tp_one, tp_two]), jnp.stack(adjoints[::-1]))

    is_last = lax.axis_index("depth") == n_depth - 1

    def relay_step(turn, top):
        bottom, unused = sweep(top)
        incoming = from_behind(bottom, "depth", -1)
        return jnp.where(is_last, seed_state, incoming)

    top_state = lax.fori_loop(0, n_depth - 1, relay_step, seed_state)
    unused_state, deflection_bar = sweep(top_state)
    abar = deflection_bar.astype(jnp.bfloat16).reshape(planes_here, 2, blocks_here, width)
    contrib = jnp.einsum("pcbr,pbrk->pbck", abar, interp, preferred_element_type=jnp.float32)
    dest = dest_tile[:, :, 0]
    order_mask = jnp.arange(blocks_here)[None, :] < jnp.arange(blocks_here)[:, None]
    same_dest = dest[:, :, None] == dest[:, None, :]
    rank = jnp.sum(jnp.logical_and(same_dest, order_mask[None]), axis=2)
    slot = dest[0] * slots + rank[0]
    send_data = jnp.zeros((n_tile * slots, 2, width), jnp.float32).at[slot].set(contrib[0])
    send_ids = jnp.zeros((n_tile * slots,), jnp.int32).at[slot].set(dest_segment[0])
    got_data = lax.all_to_all(
        send_data.reshape(n_tile, slots, 2, width), "tile", split_axis=0, concat_axis=0, tiled=True
    )
    got_ids = lax.all_to_all(
        send_ids.reshape(n_tile, slots), "tile", split_axis=0, concat_axis=0, tiled=True
    )
    summed = (
        jnp.zeros((segments, 2, width), jnp.float32)
        .at[got_ids.reshape(-1)]
        .add(got_data.reshape(-1, 2, width))
    )
    plane_maps = [jnp.transpose(summed, (1, 0, 2)).reshape(2, ROWS, COLS)]
    maps = jnp.stack(plane_maps)
    ay_ext = padded_2(maps[:, 1], (("tile", 1),), 1)
    raw = column_part(maps[:, 0]) + 0.5 * (ay_ext[:, :-2, :] - ay_ext[:, 2:, :])
    raw_ext = padded_2(raw, (("tile", 1),), 1)
    rows_done = 0.25 * raw_ext[:, :-2, :] + 0.5 * raw_ext[:, 1:-1, :] + 0.25 * raw_ext[:, 2:, :]
    return smooth_cols(rows_done)


def solution(mesh):
    return jax.shard_map(
        per_device,
        mesh=mesh,
        in_specs=(
            P("depth", None, "tile"),
            P("depth"),
            P("depth"),
            P("tile"),
            P("depth", "tile", None),
            P("depth", "tile"),
            P("depth", "tile", None, None),
        ),
        out_specs=P("depth", "tile", None),
        check_vma=False,
    )
```

profile of v0, /device:TPU:103, one launch (start us, length us, event | category | flops | bytes accessed | tf_op | source)
XLA Modules:
  0.0 640.3 jit_solution(10379709504389961642)
XLA Ops:
  12.4 5.1 all-to-all-start
  19.2 129.9 %all-reduce.4.cloned.1.call-done = f32[2,16384]{1,0:T(2,128)} async-done(((f32[2,16384]{1,0:T(2,128)}), f32[2,16384]{1,0:T(2,128)}) %all-reduce.4.cloned.1.call-update) | async-done | bytes 131088 | tf_op jit(solution)/shard_map/psum | solution.py:56
  151.7 387.7 %while.10 = (s32[]{:T(128)}, f32[4,16384]{1,0:T(4,128)S(1)}, pred[]{:T(512)}, f32[1,1,16384]{2,1,0:T(1,128)S(1)}, f32[1]{0:T(128)}, /*index=5*/f32[1,1,16384]{2,...) while((s32[]{:T(128)}, f32[4,16384]{1,0:T(4,128)S(1)}, pred[]{:T(512)}, ...), condition=%wide.region_4.5_spmd, body=%wide.region_3.4_spmd.sunk | while | flops 458754 | bytes 3342474 | solution.py:84
  153.0 2.8 collective-permute-start
  155.8 7.6 %collective-permute-done = f32[4,16384]{1,0:T(4,128)S(1)} collective-permute-done((f32[4,16384]{1,0:T(4,128)S(1)}, f32[4,16384]{1,0:T(4,128)S(1)}, u32[]{:S(2)}, u32[]{:S(2)}) %collective-permute-start) | collective-permute-done | bytes 262176 | tf_op jit(solution)/shard_map/while/body/eval_jaxpr/ppermute | solution.py:13
  164.9 1.9 collective-permute-start
  166.8 8.5 %collective-permute-done = f32[4,16384]{1,0:T(4,128)S(1)} collective-permute-done((f32[4,16384]{1,0:T(4,128)S(1)}, f32[4,16384]{1,0:T(4,128)S(1)}, u32[]{:S(2)}, u32[]{:S(2)}) %collective-permute-start) | collective-permute-done | bytes 262176 | tf_op jit(solution)/shard_map/while/body/eval_jaxpr/ppermute | solution.py:13
  176.7 1.9 collective-permute-start
  178.7 8.5 %collective-permute-done = f32[4,16384]{1,0:T(4,128)S(1)} collective-permute-done((f32[4,16384]{1,0:T(4,128)S(1)}, f32[4,16384]{1,0:T(4,128)S(1)}, u32[]{:S(2)}, u32[]{:S(2)}) %collective-permute-start) | collective-permute-done | bytes 262176 | tf_op jit(solution)/shard_map/while/body/eval_jaxpr/ppermute | solution.py:13
  188.6 1.9 collective-permute-start
  190.5 8.5 %collective-permute-done = f32[4,16384]{1,0:T(4,128)S(1)} collective-permute-done((f32[4,16384]{1,0:T(4,128)S(1)}, f32[4,16384]{1,0:T(4,128)S(1)}, u32[]{:S(2)}, u32[]{:S(2)}) %collective-permute-start) | collective-permute-done | bytes 262176 | tf_op jit(solution)/shard_map/while/body/eval_jaxpr/ppermute | solution.py:13
  200.5 1.9 collective-permute-start
  202.4 8.7 %collective-permute-done = f32[4,16384]{1,0:T(4,128)S(1)} collective-permute-done((f32[4,16384]{1,0:T(4,128)S(1)}, f32[4,16384]{1,0:T(4,128)S(1)}, u32[]{:S(2)}, u32[]{:S(2)}) %collective-permute-start) | collective-permute-done | bytes 262176 | tf_op jit(solution)/shard_map/while/body/eval_jaxpr/ppermute | solution.py:13
  212.5 1.9 collective-permute-start
  214.5 9.9 %collective-permute-done = f32[4,16384]{1,0:T(4,128)S(1)} collective-permute-done((f32[4,16384]{1,0:T(4,128)S(1)}, f32[4,16384]{1,0:T(4,128)S(1)}, u32[]{:S(2)}, u32[]{:S(2)}) %collective-permute-start) | collective-permute-done | bytes 262176 | tf_op jit(solution)/shard_map/while/body/eval_jaxpr/ppermute | solution.py:13
  225.7 1.9 collective-permute-start
  227.7 11.0 %collective-permute-done = f32[4,16384]{1,0:T(4,128)S(1)} collective-permute-done((f32[4,16384]{1,0:T(4,128)S(1)}, f32[4,16384]{1,0:T(4,128)S(1)}, u32[]{:S(2)}, u32[]{:S(2)}) %collective-permute-start) | collective-permute-done | bytes 262176 | tf_op jit(solution)/shard_map/while/body/eval_jaxpr/ppermute | solution.py:13
  240.1 1.9 collective-permute-start
  242.0 10.8 %collective-permute-done = f32[4,16384]{1,0:T(4,128)S(1)} collective-permute-done((f32[4,16384]{1,0:T(4,128)S(1)}, f32[4,16384]{1,0:T(4,128)S(1)}, u32[]{:S(2)}, u32[]{:S(2)}) %collective-permute-start) | collective-permute-done | bytes 262176 | tf_op jit(solution)/shard_map/while/body/eval_jaxpr/ppermute | solution.py:13
  254.2 1.9 collective-permute-start
  256.1 9.9 %collective-permute-done = f32[4,16384]{1,0:T(4,128)S(1)} collective-permute-done((f32[4,16384]{1,0:T(4,128)S(1)}, f32[4,16384]{1,0:T(4,128)S(1)}, u32[]{:S(2)}, u32[]{:S(2)}) %collective-permute-start) | collective-permute-done | bytes 262176 | tf_op jit(solution)/shard_map/while/body/eval_jaxpr/ppermute | solution.py:13
  267.5 1.9 collective-permute-start
  269.4 9.1 %collective-permute-done = f32[4,16384]{1,0:T(4,128)S(1)} collective-permute-done((f32[4,16384]{1,0:T(4,128)S(1)}, f32[4,16384]{1,0:T(4,128)S(1)}, u32[]{:S(2)}, u32[]{:S(2)}) %collective-permute-start) | collective-permute-done | bytes 262176 | tf_op jit(solution)/shard_map/while/body/eval_jaxpr/ppermute | solution.py:13
  279.9 1.9 collective-permute-start
  281.8 8.5 %collective-permute-done = f32[4,16384]{1,0:T(4,128)S(1)} collective-permute-done((f32[4,16384]{1,0:T(4,128)S(1)}, f32[4,16384]{1,0:T(4,128)S(1)}, u32[]{:S(2)}, u32[]{:S(2)}) %collective-permute-start) | collective-permute-done | bytes 262176 | tf_op jit(solution)/shard_map/while/body/eval_jaxpr/ppermute | solution.py:13
  291.8 1.9 collective-permute-start
  293.7 8.5 %collective-permute-done = f32[4,16384]{1,0:T(4,128)S(1)} collective-permute-done((f32[4,16384]{1,0:T(4,128)S(1)}, f32[4,16384]{1,0:T(4,128)S(1)}, u32[]{:S(2)}, u32[]{:S(2)}) %collective-permute-start) | collective-permute-done | bytes 262176 | tf_op jit(solution)/shard_map/while/body/eval_jaxpr/ppermute | solution.py:13
  303.6 1.9 collective-permute-start
  305.6 8.5 %collective-permute-done = f32[4,16384]{1,0:T(4,128)S(1)} collective-permute-done((f32[4,16384]{1,0:T(4,128)S(1)}, f32[4,16384]{1,0:T(4,128)S(1)}, u32[]{:S(2)}, u32[]{:S(2)}) %collective-permute-start) | collective-permute-done | bytes 262176 | tf_op jit(solution)/shard_map/while/body/eval_jaxpr/ppermute | solution.py:13
  315.5 1.9 collective-permute-start
  317.4 8.5 %collective-permute-done = f32[4,16384]{1,0:T(4,128)S(1)} collective-permute-done((f32[4,16384]{1,0:T(4,128)S(1)}, f32[4,16384]{1,0:T(4,128)S(1)}, u32[]{:S(2)}, u32[]{:S(2)}) %collective-permute-start) | collective-permute-done | bytes 262176 | tf_op jit(solution)/shard_map/while/body/eval_jaxpr/ppermute | solution.py:13
  327.4 1.9 collective-permute-start
  329.3 8.5 %collective-permute-done = f32[4,16384]{1,0:T(4,128)S(1)} collective-permute-done((f32[4,16384]{1,0:T(4,128)S(1)}, f32[4,16384]{1,0:T(4,128)S(1)}, u32[]{:S(2)}, u32[]{:S(2)}) %collective-permute-start) | collective-permute-done | bytes 262176 | tf_op jit(solution)/shard_map/while/body/eval_jaxpr/ppermute | solution.py:13
  339.2 1.9 collective-permute-start
  341.1 8.5 %collective-permute-done = f32[4,16384]{1,0:T(4,128)S(1)} collective-permute-done((f32[4,16384]{1,0:T(4,128)S(1)}, f32[4,16384]{1,0:T(4,128)S(1)}, u32[]{:S(2)}, u32[]{:S(2)}) %collective-permute-start) | collective-permute-done | bytes 262176 | tf_op jit(solution)/shard_map/while/body/eval_jaxpr/ppermute | solution.py:13
  351.1 1.9 collective-permute-start
  353.0 8.6 %collective-permute-done = f32[4,16384]{1,0:T(4,128)S(1)} collective-permute-done((f32[4,16384]{1,0:T(4,128)S(1)}, f32[4,16384]{1,0:T(4,128)S(1)}, u32[]{:S(2)}, u32[]{:S(2)}) %collective-permute-start) | collective-permute-done | bytes 262176 | tf_op jit(solution)/shard_map/while/body/eval_jaxpr/ppermute | solution.py:13
  365.0 9.8 %collective-permute-done = f32[4,16384]{1,0:T(4,128)S(1)} collective-permute-done((f32[4,16384]{1,0:T(4,128)S(1)}, f32[4,16384]{1,0:T(4,128)S(1)}, u32[]{:S(2)}, u32[]{:S(2)}) %collective-permute-start) | collective-permute-done | bytes 262176 | tf_op jit(solution)/shard_map/while/body/eval_jaxpr/ppermute | solution.py:13
  376.1 1.9 collective-permute-start
  378.1 10.9 %collective-permute-done = f32[4,16384]{1,0:T(4,128)S(1)} collective-permute-done((f32[4,16384]{1,0:T(4,128)S(1)}, f32[4,16384]{1,0:T(4,128)S(1)}, u32[]{:S(2)}, u32[]{:S(2)}) %collective-permute-start) | collective-permute-done | bytes 262176 | tf_op jit(solution)/shard_map/while/body/eval_jaxpr/ppermute | solution.py:13
  392.3 10.9 %collective-permute-done = f32[4,16384]{1,0:T(4,128)S(1)} collective-permute-done((f32[4,16384]{1,0:T(4,128)S(1)}, f32[4,16384]{1,0:T(4,128)S(1)}, u32[]{:S(2)}, u32[]{:S(2)}) %collective-permute-start) | collective-permute-done | bytes 262176 | tf_op jit(solution)/shard_map/while/body/eval_jaxpr/ppermute | solution.py:13
  406.6 10.0 %collective-permute-done = f32[4,16384]{1,0:T(4,128)S(1)} collective-permute-done((f32[4,16384]{1,0:T(4,128)S(1)}, f32[4,16384]{1,0:T(4,128)S(1)}, u32[]{:S(2)}, u32[]{:S(2)}) %collective-permute-start) | collective-permute-done | bytes 262176 | tf_op jit(solution)/shard_map/while/body/eval_jaxpr/ppermute | solution.py:13
  419.9 9.2 %collective-permute-done = f32[4,16384]{1,0:T(4,128)S(1)} collective-permute-done((f32[4,16384]{1,0:T(4,128)S(1)}, f32[4,16384]{1,0:T(4,128)S(1)}, u32[]{:S(2)}, u32[]{:S(2)}) %collective-permute-start) | collective-permute-done | bytes 262176 | tf_op jit(solution)/shard_map/while/body/eval_jaxpr/ppermute | solution.py:13
  432.5 8.5 %collective-permute-done = f32[4,16384]{1,0:T(4,128)S(1)} collective-permute-done((f32[4,16384]{1,0:T(4,128)S(1)}, f32[4,16384]{1,0:T(4,128)S(1)}, u32[]{:S(2)}, u32[]{:S(2)}) %collective-permute-start) | collective-permute-done | bytes 262176 | tf_op jit(solution)/shard_map/while/body/eval_jaxpr/ppermute | solution.py:13
  442.4 1.9 collective-permute-start
  444.3 8.5 %collective-permute-done = f32[4,16384]{1,0:T(4,128)S(1)} collective-permute-done((f32[4,16384]{1,0:T(4,128)S(1)}, f32[4,16384]{1,0:T(4,128)S(1)}, u32[]{:S(2)}, u32[]{:S(2)}) %collective-permute-start) | collective-permute-done | bytes 262176 | tf_op jit(solution)/shard_map/while/body/eval_jaxpr/ppermute | solution.py:13
  456.2 8.5 %collective-permute-done = f32[4,16384]{1,0:T(4,128)S(1)} collective-permute-done((f32[4,16384]{1,0:T(4,128)S(1)}, f32[4,16384]{1,0:T(4,128)S(1)}, u32[]{:S(2)}, u32[]{:S(2)}) %collective-permute-start) | collective-permute-done | bytes 262176 | tf_op jit(solution)/shard_map/while/body/eval_jaxpr/ppermute | solution.py:13
  468.0 8.5 %collective-permute-done = f32[4,16384]{1,0:T(4,128)S(1)} collective-permute-done((f32[4,16384]{1,0:T(4,128)S(1)}, f32[4,16384]{1,0:T(4,128)S(1)}, u32[]{:S(2)}, u32[]{:S(2)}) %collective-permute-start) | collective-permute-done | bytes 262176 | tf_op jit(solution)/shard_map/while/body/eval_jaxpr/ppermute | solution.py:13
  478.0 1.9 collective-permute-start
  479.9 8.5 %collective-permute-done = f32[4,16384]{1,0:T(4,128)S(1)} collective-permute-done((f32[4,16384]{1,0:T(4,128)S(1)}, f32[4,16384]{1,0:T(4,128)S(1)}, u32[]{:S(2)}, u32[]{:S(2)}) %collective-permute-start) | collective-permute-done | bytes 262176 | tf_op jit(solution)/shard_map/while/body/eval_jaxpr/ppermute | solution.py:13
  491.8 8.5 %collective-permute-done = f32[4,16384]{1,0:T(4,128)S(1)} collective-permute-done((f32[4,16384]{1,0:T(4,128)S(1)}, f32[4,16384]{1,0:T(4,128)S(1)}, u32[]{:S(2)}, u32[]{:S(2)}) %collective-permute-start) | collective-permute-done | bytes 262176 | tf_op jit(solution)/shard_map/while/body/eval_jaxpr/ppermute | solution.py:13
  503.6 8.5 %collective-permute-done = f32[4,16384]{1,0:T(4,128)S(1)} collective-permute-done((f32[4,16384]{1,0:T(4,128)S(1)}, f32[4,16384]{1,0:T(4,128)S(1)}, u32[]{:S(2)}, u32[]{:S(2)}) %collective-permute-start) | collective-permute-done | bytes 262176 | tf_op jit(solution)/shard_map/while/body/eval_jaxpr/ppermute | solution.py:13
  515.5 9.6 %collective-permute-done = f32[4,16384]{1,0:T(4,128)S(1)} collective-permute-done((f32[4,16384]{1,0:T(4,128)S(1)}, f32[4,16384]{1,0:T(4,128)S(1)}, u32[]{:S(2)}, u32[]{:S(2)}) %collective-permute-start) | collective-permute-done | bytes 262176 | tf_op jit(solution)/shard_map/while/body/eval_jaxpr/ppermute | solution.py:13
  528.5 10.8 %collective-permute-done = f32[4,16384]{1,0:T(4,128)S(1)} collective-permute-done((f32[4,16384]{1,0:T(4,128)S(1)}, f32[4,16384]{1,0:T(4,128)S(1)}, u32[]{:S(2)}, u32[]{:S(2)}) %collective-permute-start) | collective-permute-done | bytes 262176 | tf_op jit(solution)/shard_map/while/body/eval_jaxpr/ppermute | solution.py:13
  539.6 3.4 fusion.4
  543.8 12.5 %scatter_fusion = f32[256,2,128]{2,1,0:T(2,128)} fusion(f32[256,2,128]{2,1,0:T(2,128)} %broadcast.154.clone, s32[128]{0:T(128)S(1)} %fusion.14, f32[128,2,128]{2,1,0:T(2,128)S(1)} %fusion.4), kind=kCustom, calls=%fused_computation.1 | custom fusion | bytes 393728 | tf_op jit(solution)/shard_map/scatter | solution.py:93
  556.2 43.4 %all-to-all-start.1 = ((f32[8,32,2,128]{3,2,1,0:T(2,128)}), f32[8,32,2,128]{3,2,1,0:T(2,128)S(1)}, u32[]{:S(2)}, u32[]{:S(2)}) async-start(f32[8,32,2,128]{3,2,1,0:T(2,128)} %bitcast.21), calls=%async_computation.1 | async-start | bytes 524288 | tf_op jit(solution)/shard_map/all_to_all | solution.py:95
  600.9 5.2 all-to-all-done.1
  606.2 8.7 %scatter_fusion.1 = f32[256,2,128]{2,1,0:T(2,128)S(1)} fusion(f32[256,2,128]{2,1,0:T(2,128)S(1)} %broadcast.154, s32[256]{0:T(256)S(1)} %bitcast.85, f32[256,2,128]{2,1,0:T(2,128)S(1)} %bitcast.80), kind=kCustom, calls=%fused_computation.2 | custom fusion | flops 65536 | bytes 787456 | tf_op jit(solution)/shard_map/scatter-add | solution.py:104
  615.2 3.4 collective-permute-start.1
  618.6 1.9 collective-permute-start.2
  620.5 3.6 collective-permute-done.2
  626.6 2.4 collective-permute-start.4
  629.0 3.2 collective-permute-done.4
  (169 shorter events, 79.2 us)
Async XLA Ops:
  6.5 142.5 %all-reduce.4.cloned.1.call-start = ((), (), s32[]{:S(2)}) async-start(), calls=%async_computation.2 | async-start | bytes 262144 | tf_op jit(solution)/shard_map/psum | solution.py:56
  12.4 543.8 %all-to-all-start = ((s32[8,1,32]{2,1,0:T(1,128)}), s32[8,1,32]{2,1,0:T(1,128)S(1)}, u32[]{:S(2)}, u32[]{:S(2)}) async-start(s32[8,1,32]{2,1,0:T(1,128)} %all_to_all.9), calls=%async_computation | async-start | bytes 8192 | tf_op jit(solution)/shard_map/all_to_all | solution.py:98
  153.0 10.4 %collective-permute-start = (f32[4,16384]{1,0:T(4,128)S(1)}, f32[4,16384]{1,0:T(4,128)S(1)}, u32[]{:S(2)}, u32[]{:S(2)}) collective-permute-start(f32[4,16384]{1,0:T(4,128)S(1)} %pad_maximum_fusion.7), channel_id=1, source_target_pairs={{8,0},{16,8},{24,16},{32,24},{40,32},{48,40},{56,48},{64,56},{72,6... | collective-permute-start | bytes 786440 | tf_op jit(solution)/shard_map/while/body/eval_jaxpr/ppermute | solution.py:13
  164.9 10.4 %collective-permute-start = (f32[4,16384]{1,0:T(4,128)S(1)}, f32[4,16384]{1,0:T(4,128)S(1)}, u32[]{:S(2)}, u32[]{:S(2)}) collective-permute-start(f32[4,16384]{1,0:T(4,128)S(1)} %pad_maximum_fusion.7), channel_id=1, source_target_pairs={{8,0},{16,8},{24,16},{32,24},{40,32},{48,40},{56,48},{64,56},{72,6... | collective-permute-start | bytes 786440 | tf_op jit(solution)/shard_map/while/body/eval_jaxpr/ppermute | solution.py:13
  176.7 10.4 %collective-permute-start = (f32[4,16384]{1,0:T(4,128)S(1)}, f32[4,16384]{1,0:T(4,128)S(1)}, u32[]{:S(2)}, u32[]{:S(2)}) collective-permute-start(f32[4,16384]{1,0:T(4,128)S(1)} %pad_maximum_fusion.7), channel_id=1, source_target_pairs={{8,0},{16,8},{24,16},{32,24},{40,32},{48,40},{56,48},{64,56},{72,6... | collective-permute-start | bytes 786440 | tf_op jit(solution)/shard_map/while/body/eval_jaxpr/ppermute | solution.py:13
  188.6 10.4 %collective-permute-start = (f32[4,16384]{1,0:T(4,128)S(1)}, f32[4,16384]{1,0:T(4,128)S(1)}, u32[]{:S(2)}, u32[]{:S(2)}) collective-permute-start(f32[4,16384]{1,0:T(4,128)S(1)} %pad_maximum_fusion.7), channel_id=1, source_target_pairs={{8,0},{16,8},{24,16},{32,24},{40,32},{48,40},{56,48},{64,56},{72,6... | collective-permute-start | bytes 786440 | tf_op jit(solution)/shard_map/while/body/eval_jaxpr/ppermute | solution.py:13
  200.5 10.6 %collective-permute-start = (f32[4,16384]{1,0:T(4,128)S(1)}, f32[4,16384]{1,0:T(4,128)S(1)}, u32[]{:S(2)}, u32[]{:S(2)}) collective-permute-start(f32[4,16384]{1,0:T(4,128)S(1)} %pad_maximum_fusion.7), channel_id=1, source_target_pairs={{8,0},{16,8},{24,16},{32,24},{40,32},{48,40},{56,48},{64,56},{72,6... | collective-permute-start | bytes 786440 | tf_op jit(solution)/shard_map/while/body/eval_jaxpr/ppermute | solution.py:13
  212.5 11.8 %collective-permute-start = (f32[4,16384]{1,0:T(4,128)S(1)}, f32[4,16384]{1,0:T(4,128)S(1)}, u32[]{:S(2)}, u32[]{:S(2)}) collective-permute-start(f32[4,16384]{1,0:T(4,128)S(1)} %pad_maximum_fusion.7), channel_id=1, source_target_pairs={{8,0},{16,8},{24,16},{32,24},{40,32},{48,40},{56,48},{64,56},{72,6... | collective-permute-start | bytes 786440 | tf_op jit(solution)/shard_map/while/body/eval_jaxpr/ppermute | solution.py:13
  225.7 12.9 %collective-permute-start = (f32[4,16384]{1,0:T(4,128)S(1)}, f32[4,16384]{1,0:T(4,128)S(1)}, u32[]{:S(2)}, u32[]{:S(2)}) collective-permute-start(f32[4,16384]{1,0:T(4,128)S(1)} %pad_maximum_fusion.7), channel_id=1, source_target_pairs={{8,0},{16,8},{24,16},{32,24},{40,32},{48,40},{56,48},{64,56},{72,6... | collective-permute-start | bytes 786440 | tf_op jit(solution)/shard_map/while/body/eval_jaxpr/ppermute | solution.py:13
  240.1 12.7 %collective-permute-start = (f32[4,16384]{1,0:T(4,128)S(1)}, f32[4,16384]{1,0:T(4,128)S(1)}, u32[]{:S(2)}, u32[]{:S(2)}) collective-permute-start(f32[4,16384]{1,0:T(4,128)S(1)} %pad_maximum_fusion.7), channel_id=1, source_target_pairs={{8,0},{16,8},{24,16},{32,24},{40,32},{48,40},{56,48},{64,56},{72,6... | collective-permute-start | bytes 786440 | tf_op jit(solution)/shard_map/while/body/eval_jaxpr/ppermute | solution.py:13
  254.2 11.9 %collective-permute-start = (f32[4,16384]{1,0:T(4,128)S(1)}, f32[4,16384]{1,0:T(4,128)S(1)}, u32[]{:S(2)}, u32[]{:S(2)}) collective-permute-start(f32[4,16384]{1,0:T(4,128)S(1)} %pad_maximum_fusion.7), channel_id=1, source_target_pairs={{8,0},{16,8},{24,16},{32,24},{40,32},{48,40},{56,48},{64,56},{72,6... | collective-permute-start | bytes 786440 | tf_op jit(solution)/shard_map/while/body/eval_jaxpr/ppermute | solution.py:13
  267.5 11.0 %collective-permute-start = (f32[4,16384]{1,0:T(4,128)S(1)}, f32[4,16384]{1,0:T(4,128)S(1)}, u32[]{:S(2)}, u32[]{:S(2)}) collective-permute-start(f32[4,16384]{1,0:T(4,128)S(1)} %pad_maximum_fusion.7), channel_id=1, source_target_pairs={{8,0},{16,8},{24,16},{32,24},{40,32},{48,40},{56,48},{64,56},{72,6... | collective-permute-start | bytes 786440 | tf_op jit(solution)/shard_map/while/body/eval_jaxpr/ppermute | solution.py:13
  279.9 10.4 %collective-permute-start = (f32[4,16384]{1,0:T(4,128)S(1)}, f32[4,16384]{1,0:T(4,128)S(1)}, u32[]{:S(2)}, u32[]{:S(2)}) collective-permute-start(f32[4,16384]{1,0:T(4,128)S(1)} %pad_maximum_fusion.7), channel_id=1, source_target_pairs={{8,0},{16,8},{24,16},{32,24},{40,32},{48,40},{56,48},{64,56},{72,6... | collective-permute-start | bytes 786440 | tf_op jit(solution)/shard_map/while/body/eval_jaxpr/ppermute | solution.py:13
  291.8 10.4 %collective-permute-start = (f32[4,16384]{1,0:T(4,128)S(1)}, f32[4,16384]{1,0:T(4,128)S(1)}, u32[]{:S(2)}, u32[]{:S(2)}) collective-permute-start(f32[4,16384]{1,0:T(4,128)S(1)} %pad_maximum_fusion.7), channel_id=1, source_target_pairs={{8,0},{16,8},{24,16},{32,24},{40,32},{48,40},{56,48},{64,56},{72,6... | collective-permute-start | bytes 786440 | tf_op jit(solution)/shard_map/while/body/eval_jaxpr/ppermute | solution.py:13
  303.6 10.4 %collective-permute-start = (f32[4,16384]{1,0:T(4,128)S(1)}, f32[4,16384]{1,0:T(4,128)S(1)}, u32[]{:S(2)}, u32[]{:S(2)}) collective-permute-start(f32[4,16384]{1,0:T(4,128)S(1)} %pad_maximum_fusion.7), channel_id=1, source_target_pairs={{8,0},{16,8},{24,16},{32,24},{40,32},{48,40},{56,48},{64,56},{72,6... | collective-permute-start | bytes 786440 | tf_op jit(solution)/shard_map/while/body/eval_jaxpr/ppermute | solution.py:13
  315.5 10.4 %collective-permute-start = (f32[4,16384]{1,0:T(4,128)S(1)}, f32[4,16384]{1,0:T(4,128)S(1)}, u32[]{:S(2)}, u32[]{:S(2)}) collective-permute-start(f32[4,16384]{1,0:T(4,128)S(1)} %pad_maximum_fusion.7), channel_id=1, source_target_pairs={{8,0},{16,8},{24,16},{32,24},{40,32},{48,40},{56,48},{64,56},{72,6... | collective-permute-start | bytes 786440 | tf_op jit(solution)/shard_map/while/body/eval_jaxpr/ppermute | solution.py:13
  327.4 10.4 %collective-permute-start = (f32[4,16384]{1,0:T(4,128)S(1)}, f32[4,16384]{1,0:T(4,128)S(1)}, u32[]{:S(2)}, u32[]{:S(2)}) collective-permute-start(f32[4,16384]{1,0:T(4,128)S(1)} %pad_maximum_fusion.7), channel_id=1, source_target_pairs={{8,0},{16,8},{24,16},{32,24},{40,32},{48,40},{56,48},{64,56},{72,6... | collective-permute-start | bytes 786440 | tf_op jit(solution)/shard_map/while/body/eval_jaxpr/ppermute | solution.py:13
  339.2 10.4 %collective-permute-start = (f32[4,16384]{1,0:T(4,128)S(1)}, f32[4,16384]{1,0:T(4,128)S(1)}, u32[]{:S(2)}, u32[]{:S(2)}) collective-permute-start(f32[4,16384]{1,0:T(4,128)S(1)} %pad_maximum_fusion.7), channel_id=1, source_target_pairs={{8,0},{16,8},{24,16},{32,24},{40,32},{48,40},{56,48},{64,56},{72,6... | collective-permute-start | bytes 786440 | tf_op jit(solution)/shard_map/while/body/eval_jaxpr/ppermute | solution.py:13
  351.1 10.5 %collective-permute-start = (f32[4,16384]{1,0:T(4,128)S(1)}, f32[4,16384]{1,0:T(4,128)S(1)}, u32[]{:S(2)}, u32[]{:S(2)}) collective-permute-start(f32[4,16384]{1,0:T(4,128)S(1)} %pad_maximum_fusion.7), channel_id=1, source_target_pairs={{8,0},{16,8},{24,16},{32,24},{40,32},{48,40},{56,48},{64,56},{72,6... | collective-permute-start | bytes 786440 | tf_op jit(solution)/shard_map/while/body/eval_jaxpr/ppermute | solution.py:13
  363.0 11.7 %collective-permute-start = (f32[4,16384]{1,0:T(4,128)S(1)}, f32[4,16384]{1,0:T(4,128)S(1)}, u32[]{:S(2)}, u32[]{:S(2)}) collective-permute-start(f32[4,16384]{1,0:T(4,128)S(1)} %pad_maximum_fusion.7), channel_id=1, source_target_pairs={{8,0},{16,8},{24,16},{32,24},{40,32},{48,40},{56,48},{64,56},{72,6... | collective-permute-start | bytes 786440 | tf_op jit(solution)/shard_map/while/body/eval_jaxpr/ppermute | solution.py:13
  376.1 12.8 %collective-permute-start = (f32[4,16384]{1,0:T(4,128)S(1)}, f32[4,16384]{1,0:T(4,128)S(1)}, u32[]{:S(2)}, u32[]{:S(2)}) collective-permute-start(f32[4,16384]{1,0:T(4,128)S(1)} %pad_maximum_fusion.7), channel_id=1, source_target_pairs={{8,0},{16,8},{24,16},{32,24},{40,32},{48,40},{56,48},{64,56},{72,6... | collective-permute-start | bytes 786440 | tf_op jit(solution)/shard_map/while/body/eval_jaxpr/ppermute | solution.py:13
  390.4 12.8 %collective-permute-start = (f32[4,16384]{1,0:T(4,128)S(1)}, f32[4,16384]{1,0:T(4,128)S(1)}, u32[]{:S(2)}, u32[]{:S(2)}) collective-permute-start(f32[4,16384]{1,0:T(4,128)S(1)} %pad_maximum_fusion.7), channel_id=1, source_target_pairs={{8,0},{16,8},{24,16},{32,24},{40,32},{48,40},{56,48},{64,56},{72,6... | collective-permute-start | bytes 786440 | tf_op jit(solution)/shard_map/while/body/eval_jaxpr/ppermute | solution.py:13
  404.6 12.0 %collective-permute-start = (f32[4,16384]{1,0:T(4,128)S(1)}, f32[4,16384]{1,0:T(4,128)S(1)}, u32[]{:S(2)}, u32[]{:S(2)}) collective-permute-start(f32[4,16384]{1,0:T(4,128)S(1)} %pad_maximum_fusion.7), channel_id=1, source_target_pairs={{8,0},{16,8},{24,16},{32,24},{40,32},{48,40},{56,48},{64,56},{72,6... | collective-permute-start | bytes 786440 | tf_op jit(solution)/shard_map/while/body/eval_jaxpr/ppermute | solution.py:13
  418.0 11.1 %collective-permute-start = (f32[4,16384]{1,0:T(4,128)S(1)}, f32[4,16384]{1,0:T(4,128)S(1)}, u32[]{:S(2)}, u32[]{:S(2)}) collective-permute-start(f32[4,16384]{1,0:T(4,128)S(1)} %pad_maximum_fusion.7), channel_id=1, source_target_pairs={{8,0},{16,8},{24,16},{32,24},{40,32},{48,40},{56,48},{64,56},{72,6... | collective-permute-start | bytes 786440 | tf_op jit(solution)/shard_map/while/body/eval_jaxpr/ppermute | solution.py:13
  430.5 10.4 %collective-permute-start = (f32[4,16384]{1,0:T(4,128)S(1)}, f32[4,16384]{1,0:T(4,128)S(1)}, u32[]{:S(2)}, u32[]{:S(2)}) collective-permute-start(f32[4,16384]{1,0:T(4,128)S(1)} %pad_maximum_fusion.7), channel_id=1, source_target_pairs={{8,0},{16,8},{24,16},{32,24},{40,32},{48,40},{56,48},{64,56},{72,6... | collective-permute-start | bytes 786440 | tf_op jit(solution)/shard_map/while/body/eval_jaxpr/ppermute | solution.py:13
  442.4 10.4 %collective-permute-start = (f32[4,16384]{1,0:T(4,128)S(1)}, f32[4,16384]{1,0:T(4,128)S(1)}, u32[]{:S(2)}, u32[]{:S(2)}) collective-permute-start(f32[4,16384]{1,0:T(4,128)S(1)} %pad_maximum_fusion.7), channel_id=1, source_target_pairs={{8,0},{16,8},{24,16},{32,24},{40,32},{48,40},{56,48},{64,56},{72,6... | collective-permute-start | bytes 786440 | tf_op jit(solution)/shard_map/while/body/eval_jaxpr/ppermute | solution.py:13
  454.3 10.4 %collective-permute-start = (f32[4,16384]{1,0:T(4,128)S(1)}, f32[4,16384]{1,0:T(4,128)S(1)}, u32[]{:S(2)}, u32[]{:S(2)}) collective-permute-start(f32[4,16384]{1,0:T(4,128)S(1)} %pad_maximum_fusion.7), channel_id=1, source_target_pairs={{8,0},{16,8},{24,16},{32,24},{40,32},{48,40},{56,48},{64,56},{72,6... | collective-permute-start | bytes 786440 | tf_op jit(solution)/shard_map/while/body/eval_jaxpr/ppermute | solution.py:13
  466.1 10.4 %collective-permute-start = (f32[4,16384]{1,0:T(4,128)S(1)}, f32[4,16384]{1,0:T(4,128)S(1)}, u32[]{:S(2)}, u32[]{:S(2)}) collective-permute-start(f32[4,16384]{1,0:T(4,128)S(1)} %pad_maximum_fusion.7), channel_id=1, source_target_pairs={{8,0},{16,8},{24,16},{32,24},{40,32},{48,40},{56,48},{64,56},{72,6... | collective-permute-start | bytes 786440 | tf_op jit(solution)/shard_map/while/body/eval_jaxpr/ppermute | solution.py:13
  478.0 10.4 %collective-permute-start = (f32[4,16384]{1,0:T(4,128)S(1)}, f32[4,16384]{1,0:T(4,128)S(1)}, u32[]{:S(2)}, u32[]{:S(2)}) collective-permute-start(f32[4,16384]{1,0:T(4,128)S(1)} %pad_maximum_fusion.7), channel_id=1, source_target_pairs={{8,0},{16,8},{24,16},{32,24},{40,32},{48,40},{56,48},{64,56},{72,6... | collective-permute-start | bytes 786440 | tf_op jit(solution)/shard_map/while/body/eval_jaxpr/ppermute | solution.py:13
  489.8 10.4 %collective-permute-start = (f32[4,16384]{1,0:T(4,128)S(1)}, f32[4,16384]{1,0:T(4,128)S(1)}, u32[]{:S(2)}, u32[]{:S(2)}) collective-permute-start(f32[4,16384]{1,0:T(4,128)S(1)} %pad_maximum_fusion.7), channel_id=1, source_target_pairs={{8,0},{16,8},{24,16},{32,24},{40,32},{48,40},{56,48},{64,56},{72,6... | collective-permute-start | bytes 786440 | tf_op jit(solution)/shard_map/while/body/eval_jaxpr/ppermute | solution.py:13
  501.7 10.4 %collective-permute-start = (f32[4,16384]{1,0:T(4,128)S(1)}, f32[4,16384]{1,0:T(4,128)S(1)}, u32[]{:S(2)}, u32[]{:S(2)}) collective-permute-start(f32[4,16384]{1,0:T(4,128)S(1)} %pad_maximum_fusion.7), channel_id=1, source_target_pairs={{8,0},{16,8},{24,16},{32,24},{40,32},{48,40},{56,48},{64,56},{72,6... | collective-permute-start | bytes 786440 | tf_op jit(solution)/shard_map/while/body/eval_jaxpr/ppermute | solution.py:13
  513.6 11.6 %collective-permute-start = (f32[4,16384]{1,0:T(4,128)S(1)}, f32[4,16384]{1,0:T(4,128)S(1)}, u32[]{:S(2)}, u32[]{:S(2)}) collective-permute-start(f32[4,16384]{1,0:T(4,128)S(1)} %pad_maximum_fusion.7), channel_id=1, source_target_pairs={{8,0},{16,8},{24,16},{32,24},{40,32},{48,40},{56,48},{64,56},{72,6... | collective-permute-start | bytes 786440 | tf_op jit(solution)/shard_map/while/body/eval_jaxpr/ppermute | solution.py:13
  526.6 12.7 %collective-permute-start = (f32[4,16384]{1,0:T(4,128)S(1)}, f32[4,16384]{1,0:T(4,128)S(1)}, u32[]{:S(2)}, u32[]{:S(2)}) collective-permute-start(f32[4,16384]{1,0:T(4,128)S(1)} %pad_maximum_fusion.7), channel_id=1, source_target_pairs={{8,0},{16,8},{24,16},{32,24},{40,32},{48,40},{56,48},{64,56},{72,6... | collective-permute-start | bytes 786440 | tf_op jit(solution)/shard_map/while/body/eval_jaxpr/ppermute | solution.py:13
  556.2 49.9 %all-to-all-start.1 = ((f32[8,32,2,128]{3,2,1,0:T(2,128)}), f32[8,32,2,128]{3,2,1,0:T(2,128)S(1)}, u32[]{:S(2)}, u32[]{:S(2)}) async-start(f32[8,32,2,128]{3,2,1,0:T(2,128)} %bitcast.21), calls=%async_computation.1 | async-start | bytes 524288 | tf_op jit(solution)/shard_map/all_to_all | solution.py:95
  615.2 5.3 collective-permute-start.1
  618.6 5.6 collective-permute-start.2
  624.7 4.3 collective-permute-start.3
  626.6 5.6 collective-permute-start.4
Sparse Core Ops, SparseCore 0:
  10.8 138.2 all-reduce.3
where the time goes:
time: 642 us; the launch traced here: 640 us
  waiting for transfers between devices  425 us (66%)
  starting transfers between devices  119 us (19%)
  other arithmetic  60.1 us (9%)
  local copies, waits for them, and re-layouts  17.1 us (3%)
  between operations  14.9 us (2%)
    ppermute x31, waiting for transfers between devices, from_behind(): lax.ppermute(value, axis, [(source, source + steps) for source in range(l...  283 us
    psum x1, waiting for transfers between devices, per_device(): shear = lax.psum(local_terms, 'depth')  130 us
    ppermute x31, starting transfers between devices, from_behind(): lax.ppermute(value, axis, [(source, source + steps) for source in range(l...  60.4 us
    all_to_all x1, starting transfers between devices, per_device(): lax.all_to_all(send_data.reshape(n_tile, slots, 2, width), 'tile', split_...  43.4 us
    sub x31, other arithmetic, sweep(): new_one = xb_one - (jxx[0] * tp_one + jxy[0] * tp_two)  27.6 us
  transfers between devices with their start and end apart: 38, of which 35 were waited for; matrix products, arithmetic and copies ran while one was open for 11% of the time, Pallas kernels for 0%

commit v1 on v0

--- a/solution.py
+++ b/solution.py
@@ -53,7 +53,7 @@
             -jnp.sum(plane_weight[:, None] * jxy, axis=0),
         ]
     )
-    shear = lax.psum(local_terms, "depth")
+    shear = jnp.sum(lax.all_gather(local_terms, "depth"), axis=0)
     cross = -shear[0] * jnp.sin(2.0 * ray_angle) + shear[1] * jnp.cos(2.0 * ray_angle)
     seed_state = jnp.stack(
         [

time: 642 us -> 580 us (0.903)
  waiting for transfers between devices: 425 us -> 362 us
    psum x1 -> x0, waiting for transfers between devices: 130 us -> none  [per_device(): shear = lax.psum(local_terms, 'depth')]
    all_gather x0 -> x1, waiting for transfers between devices: none -> 67.7 us  [per_device(): shear = jnp.sum(lax.all_gather(local_terms, 'depth'), axis=0)]
  transfers between devices with their start and end apart: 38 -> 38, of which waited for: 35 -> 35; matrix products, arithmetic and copies ran while one was open for 11% -> 12% of each run, Pallas kernels for 0% -> 0%
where the time goes in v1:
time: 580 us; the launch traced here: 578 us
  waiting for transfers between devices  362 us (62%)
  starting transfers between devices  117 us (20%)
  other arithmetic  61.9 us (11%)
  local copies, waits for them, and re-layouts  17.1 us (3%)
  between operations  14.9 us (3%)
    ppermute x31, waiting for transfers between devices, from_behind(): lax.ppermute(value, axis, [(source, source + steps) for source in range(l...  282 us
    all_gather x1, waiting for transfers between devices, per_device(): shear = jnp.sum(lax.all_gather(local_terms, 'depth'), axis=0)  67.7 us
    ppermute x31, starting transfers between devices, from_behind(): lax.ppermute(value, axis, [(source, source + steps) for source in range(l...  60.2 us
    all_to_all x1, starting transfers between devices, per_device(): lax.all_to_all(send_data.reshape(n_tile, slots, 2, width), 'tile', split_...  42.5 us
    sub x31, other arithmetic, sweep(): new_one = xb_one - (jxx[0] * tp_one + jxy[0] * tp_two)  27.6 us
    scatter x1, local copies, waits for them, and re-layouts, per_device(): jnp.zeros((n_tile * slots, 2, width), jnp.float32).at[slot].set(contrib[0])  12.5 us
  transfers between devices with their start and end apart: 38, of which 35 were waited for; matrix products, arithmetic and copies ran while one was open for 12% of the time, Pallas kernels for 0%

profile of v1, /device:TPU:103, one launch (start us, length us, event | category | flops | bytes accessed | tf_op | source)
XLA Modules:
  0.0 577.9 jit_solution(6432754596403429686)
XLA Ops:
  12.4 5.1 all-to-all-start
  19.2 67.7 %all-gather.4.cloned.1.call-done = f32[32,2,16384]{2,1,0:T(2,128)} async-done(((f32[1,2,16384]{2,1,0:T(2,128)}), f32[32,2,16384]{2,1,0:T(2,128)}) %all-gather.4.cloned.1.call-update) | async-done | bytes 4194320 | tf_op jit(solution)/shard_map/all_gather | solution.py:56
  86.9 3.6 reduce_sum.23
  91.3 386.6 %while.10 = (s32[]{:T(128)}, f32[4,16384]{1,0:T(4,128)S(1)}, pred[]{:T(512)}, f32[1,1,16384]{2,1,0:T(1,128)S(1)}, f32[1]{0:T(128)}, /*index=5*/f32[1,1,16384]{2,...) while((s32[]{:T(128)}, f32[4,16384]{1,0:T(4,128)S(1)}, pred[]{:T(512)}, ...), condition=%wide.region_4.5_spmd, body=%wide.region_3.4_spmd.sunk | while | flops 458754 | bytes 3342474 | solution.py:84
  92.6 2.6 collective-permute-start
  95.2 7.9 %collective-permute-done = f32[4,16384]{1,0:T(4,128)S(1)} collective-permute-done((f32[4,16384]{1,0:T(4,128)S(1)}, f32[4,16384]{1,0:T(4,128)S(1)}, u32[]{:S(2)}, u32[]{:S(2)}) %collective-permute-start) | collective-permute-done | bytes 262176 | tf_op jit(solution)/shard_map/while/body/eval_jaxpr/ppermute | solution.py:13
  104.5 1.9 collective-permute-start
  106.4 8.5 %collective-permute-done = f32[4,16384]{1,0:T(4,128)S(1)} collective-permute-done((f32[4,16384]{1,0:T(4,128)S(1)}, f32[4,16384]{1,0:T(4,128)S(1)}, u32[]{:S(2)}, u32[]{:S(2)}) %collective-permute-start) | collective-permute-done | bytes 262176 | tf_op jit(solution)/shard_map/while/body/eval_jaxpr/ppermute | solution.py:13
  116.3 1.9 collective-permute-start
  118.3 8.5 %collective-permute-done = f32[4,16384]{1,0:T(4,128)S(1)} collective-permute-done((f32[4,16384]{1,0:T(4,128)S(1)}, f32[4,16384]{1,0:T(4,128)S(1)}, u32[]{:S(2)}, u32[]{:S(2)}) %collective-permute-start) | collective-permute-done | bytes 262176 | tf_op jit(solution)/shard_map/while/body/eval_jaxpr/ppermute | solution.py:13
  128.2 1.9 collective-permute-start
  130.1 8.5 %collective-permute-done = f32[4,16384]{1,0:T(4,128)S(1)} collective-permute-done((f32[4,16384]{1,0:T(4,128)S(1)}, f32[4,16384]{1,0:T(4,128)S(1)}, u32[]{:S(2)}, u32[]{:S(2)}) %collective-permute-start) | collective-permute-done | bytes 262176 | tf_op jit(solution)/shard_map/while/body/eval_jaxpr/ppermute | solution.py:13
  140.1 1.9 collective-permute-start
  142.0 8.5 %collective-permute-done = f32[4,16384]{1,0:T(4,128)S(1)} collective-permute-done((f32[4,16384]{1,0:T(4,128)S(1)}, f32[4,16384]{1,0:T(4,128)S(1)}, u32[]{:S(2)}, u32[]{:S(2)}) %collective-permute-start) | collective-permute-done | bytes 262176 | tf_op jit(solution)/shard_map/while/body/eval_jaxpr/ppermute | solution.py:13
  151.9 1.9 collective-permute-start
  153.8 9.1 %collective-permute-done = f32[4,16384]{1,0:T(4,128)S(1)} collective-permute-done((f32[4,16384]{1,0:T(4,128)S(1)}, f32[4,16384]{1,0:T(4,128)S(1)}, u32[]{:S(2)}, u32[]{:S(2)}) %collective-permute-start) | collective-permute-done | bytes 262176 | tf_op jit(solution)/shard_map/while/body/eval_jaxpr/ppermute | solution.py:13
  164.4 1.9 collective-permute-start
  166.3 10.3 %collective-permute-done = f32[4,16384]{1,0:T(4,128)S(1)} collective-permute-done((f32[4,16384]{1,0:T(4,128)S(1)}, f32[4,16384]{1,0:T(4,128)S(1)}, u32[]{:S(2)}, u32[]{:S(2)}) %collective-permute-start) | collective-permute-done | bytes 262176 | tf_op jit(solution)/shard_map/while/body/eval_jaxpr/ppermute | solution.py:13
  178.0 1.9 collective-permute-start
  180.0 11.5 %collective-permute-done = f32[4,16384]{1,0:T(4,128)S(1)} collective-permute-done((f32[4,16384]{1,0:T(4,128)S(1)}, f32[4,16384]{1,0:T(4,128)S(1)}, u32[]{:S(2)}, u32[]{:S(2)}) %collective-permute-start) | collective-permute-done | bytes 262176 | tf_op jit(solution)/shard_map/while/body/eval_jaxpr/ppermute | solution.py:13
  192.9 1.9 collective-permute-start
  194.8 10.6 %collective-permute-done = f32[4,16384]{1,0:T(4,128)S(1)} collective-permute-done((f32[4,16384]{1,0:T(4,128)S(1)}, f32[4,16384]{1,0:T(4,128)S(1)}, u32[]{:S(2)}, u32[]{:S(2)}) %collective-permute-start) | collective-permute-done | bytes 262176 | tf_op jit(solution)/shard_map/while/body/eval_jaxpr/ppermute | solution.py:13
  206.9 1.9 collective-permute-start
  208.8 9.8 %collective-permute-done = f32[4,16384]{1,0:T(4,128)S(1)} collective-permute-done((f32[4,16384]{1,0:T(4,128)S(1)}, f32[4,16384]{1,0:T(4,128)S(1)}, u32[]{:S(2)}, u32[]{:S(2)}) %collective-permute-start) | collective-permute-done | bytes 262176 | tf_op jit(solution)/shard_map/while/body/eval_jaxpr/ppermute | solution.py:13
  220.0 1.9 collective-permute-start
  222.0 8.9 %collective-permute-done = f32[4,16384]{1,0:T(4,128)S(1)} collective-permute-done((f32[4,16384]{1,0:T(4,128)S(1)}, f32[4,16384]{1,0:T(4,128)S(1)}, u32[]{:S(2)}, u32[]{:S(2)}) %collective-permute-start) | collective-permute-done | bytes 262176 | tf_op jit(solution)/shard_map/while/body/eval_jaxpr/ppermute | solution.py:13
  232.3 1.9 collective-permute-start
  234.2 8.5 %collective-permute-done = f32[4,16384]{1,0:T(4,128)S(1)} collective-permute-done((f32[4,16384]{1,0:T(4,128)S(1)}, f32[4,16384]{1,0:T(4,128)S(1)}, u32[]{:S(2)}, u32[]{:S(2)}) %collective-permute-start) | collective-permute-done | bytes 262176 | tf_op jit(solution)/shard_map/while/body/eval_jaxpr/ppermute | solution.py:13
  244.2 1.9 collective-permute-start
  246.1 8.5 %collective-permute-done = f32[4,16384]{1,0:T(4,128)S(1)} collective-permute-done((f32[4,16384]{1,0:T(4,128)S(1)}, f32[4,16384]{1,0:T(4,128)S(1)}, u32[]{:S(2)}, u32[]{:S(2)}) %collective-permute-start) | collective-permute-done | bytes 262176 | tf_op jit(solution)/shard_map/while/body/eval_jaxpr/ppermute | solution.py:13
  256.0 1.9 collective-permute-start
  258.0 8.5 %collective-permute-done = f32[4,16384]{1,0:T(4,128)S(1)} collective-permute-done((f32[4,16384]{1,0:T(4,128)S(1)}, f32[4,16384]{1,0:T(4,128)S(1)}, u32[]{:S(2)}, u32[]{:S(2)}) %collective-permute-start) | collective-permute-done | bytes 262176 | tf_op jit(solution)/shard_map/while/body/eval_jaxpr/ppermute | solution.py:13
  269.8 8.5 %collective-permute-done = f32[4,16384]{1,0:T(4,128)S(1)} collective-permute-done((f32[4,16384]{1,0:T(4,128)S(1)}, f32[4,16384]{1,0:T(4,128)S(1)}, u32[]{:S(2)}, u32[]{:S(2)}) %collective-permute-start) | collective-permute-done | bytes 262176 | tf_op jit(solution)/shard_map/while/body/eval_jaxpr/ppermute | solution.py:13
  279.8 1.9 collective-permute-start
  281.7 8.5 %collective-permute-done = f32[4,16384]{1,0:T(4,128)S(1)} collective-permute-done((f32[4,16384]{1,0:T(4,128)S(1)}, f32[4,16384]{1,0:T(4,128)S(1)}, u32[]{:S(2)}, u32[]{:S(2)}) %collective-permute-start) | collective-permute-done | bytes 262176 | tf_op jit(solution)/shard_map/while/body/eval_jaxpr/ppermute | solution.py:13
  293.6 8.5 %collective-permute-done = f32[4,16384]{1,0:T(4,128)S(1)} collective-permute-done((f32[4,16384]{1,0:T(4,128)S(1)}, f32[4,16384]{1,0:T(4,128)S(1)}, u32[]{:S(2)}, u32[]{:S(2)}) %collective-permute-start) | collective-permute-done | bytes 262176 | tf_op jit(solution)/shard_map/while/body/eval_jaxpr/ppermute | solution.py:13
  305.4 8.7 %collective-permute-done = f32[4,16384]{1,0:T(4,128)S(1)} collective-permute-done((f32[4,16384]{1,0:T(4,128)S(1)}, f32[4,16384]{1,0:T(4,128)S(1)}, u32[]{:S(2)}, u32[]{:S(2)}) %collective-permute-start) | collective-permute-done | bytes 262176 | tf_op jit(solution)/shard_map/while/body/eval_jaxpr/ppermute | solution.py:13
  317.5 9.9 %collective-permute-done = f32[4,16384]{1,0:T(4,128)S(1)} collective-permute-done((f32[4,16384]{1,0:T(4,128)S(1)}, f32[4,16384]{1,0:T(4,128)S(1)}, u32[]{:S(2)}, u32[]{:S(2)}) %collective-permute-start) | collective-permute-done | bytes 262176 | tf_op jit(solution)/shard_map/while/body/eval_jaxpr/ppermute | solution.py:13
  330.7 11.0 %collective-permute-done = f32[4,16384]{1,0:T(4,128)S(1)} collective-permute-done((f32[4,16384]{1,0:T(4,128)S(1)}, f32[4,16384]{1,0:T(4,128)S(1)}, u32[]{:S(2)}, u32[]{:S(2)}) %collective-permute-start) | collective-permute-done | bytes 262176 | tf_op jit(solution)/shard_map/while/body/eval_jaxpr/ppermute | solution.py:13
  345.1 10.8 %collective-permute-done = f32[4,16384]{1,0:T(4,128)S(1)} collective-permute-done((f32[4,16384]{1,0:T(4,128)S(1)}, f32[4,16384]{1,0:T(4,128)S(1)}, u32[]{:S(2)}, u32[]{:S(2)}) %collective-permute-start) | collective-permute-done | bytes 262176 | tf_op jit(solution)/shard_map/while/body/eval_jaxpr/ppermute | solution.py:13
  357.3 1.9 collective-permute-start
  359.2 9.9 %collective-permute-done = f32[4,16384]{1,0:T(4,128)S(1)} collective-permute-done((f32[4,16384]{1,0:T(4,128)S(1)}, f32[4,16384]{1,0:T(4,128)S(1)}, u32[]{:S(2)}, u32[]{:S(2)}) %collective-permute-start) | collective-permute-done | bytes 262176 | tf_op jit(solution)/shard_map/while/body/eval_jaxpr/ppermute | solution.py:13
  372.5 9.0 %collective-permute-done = f32[4,16384]{1,0:T(4,128)S(1)} collective-permute-done((f32[4,16384]{1,0:T(4,128)S(1)}, f32[4,16384]{1,0:T(4,128)S(1)}, u32[]{:S(2)}, u32[]{:S(2)}) %collective-permute-start) | collective-permute-done | bytes 262176 | tf_op jit(solution)/shard_map/while/body/eval_jaxpr/ppermute | solution.py:13
  384.9 8.5 %collective-permute-done = f32[4,16384]{1,0:T(4,128)S(1)} collective-permute-done((f32[4,16384]{1,0:T(4,128)S(1)}, f32[4,16384]{1,0:T(4,128)S(1)}, u32[]{:S(2)}, u32[]{:S(2)}) %collective-permute-start) | collective-permute-done | bytes 262176 | tf_op jit(solution)/shard_map/while/body/eval_jaxpr/ppermute | solution.py:13
  396.7 8.5 %collective-permute-done = f32[4,16384]{1,0:T(4,128)S(1)} collective-permute-done((f32[4,16384]{1,0:T(4,128)S(1)}, f32[4,16384]{1,0:T(4,128)S(1)}, u32[]{:S(2)}, u32[]{:S(2)}) %collective-permute-start) | collective-permute-done | bytes 262176 | tf_op jit(solution)/shard_map/while/body/eval_jaxpr/ppermute | solution.py:13
  408.6 8.5 %collective-permute-done = f32[4,16384]{1,0:T(4,128)S(1)} collective-permute-done((f32[4,16384]{1,0:T(4,128)S(1)}, f32[4,16384]{1,0:T(4,128)S(1)}, u32[]{:S(2)}, u32[]{:S(2)}) %collective-permute-start) | collective-permute-done | bytes 262176 | tf_op jit(solution)/shard_map/while/body/eval_jaxpr/ppermute | solution.py:13
  418.5 1.9 collective-permute-start
  420.5 8.5 %collective-permute-done = f32[4,16384]{1,0:T(4,128)S(1)} collective-permute-done((f32[4,16384]{1,0:T(4,128)S(1)}, f32[4,16384]{1,0:T(4,128)S(1)}, u32[]{:S(2)}, u32[]{:S(2)}) %collective-permute-start) | collective-permute-done | bytes 262176 | tf_op jit(solution)/shard_map/while/body/eval_jaxpr/ppermute | solution.py:13
  432.3 8.5 %collective-permute-done = f32[4,16384]{1,0:T(4,128)S(1)} collective-permute-done((f32[4,16384]{1,0:T(4,128)S(1)}, f32[4,16384]{1,0:T(4,128)S(1)}, u32[]{:S(2)}, u32[]{:S(2)}) %collective-permute-start) | collective-permute-done | bytes 262176 | tf_op jit(solution)/shard_map/while/body/eval_jaxpr/ppermute | solution.py:13
  444.2 8.5 %collective-permute-done = f32[4,16384]{1,0:T(4,128)S(1)} collective-permute-done((f32[4,16384]{1,0:T(4,128)S(1)}, f32[4,16384]{1,0:T(4,128)S(1)}, u32[]{:S(2)}, u32[]{:S(2)}) %collective-permute-start) | collective-permute-done | bytes 262176 | tf_op jit(solution)/shard_map/while/body/eval_jaxpr/ppermute | solution.py:13
  454.1 1.9 collective-permute-start
  456.1 8.6 %collective-permute-done = f32[4,16384]{1,0:T(4,128)S(1)} collective-permute-done((f32[4,16384]{1,0:T(4,128)S(1)}, f32[4,16384]{1,0:T(4,128)S(1)}, u32[]{:S(2)}, u32[]{:S(2)}) %collective-permute-start) | collective-permute-done | bytes 262176 | tf_op jit(solution)/shard_map/while/body/eval_jaxpr/ppermute | solution.py:13
  466.1 1.9 collective-permute-start
  468.0 9.8 %collective-permute-done = f32[4,16384]{1,0:T(4,128)S(1)} collective-permute-done((f32[4,16384]{1,0:T(4,128)S(1)}, f32[4,16384]{1,0:T(4,128)S(1)}, u32[]{:S(2)}, u32[]{:S(2)}) %collective-permute-start) | collective-permute-done | bytes 262176 | tf_op jit(solution)/shard_map/while/body/eval_jaxpr/ppermute | solution.py:13
  478.1 3.4 fusion.4
  482.3 12.5 %scatter_fusion = f32[256,2,128]{2,1,0:T(2,128)} fusion(f32[256,2,128]{2,1,0:T(2,128)} %broadcast.154.clone, s32[128]{0:T(128)S(1)} %fusion.14, f32[128,2,128]{2,1,0:T(2,128)S(1)} %fusion.4), kind=kCustom, calls=%fused_computation.1 | custom fusion | bytes 393728 | tf_op jit(solution)/shard_map/scatter | solution.py:93
  494.8 42.5 %all-to-all-start.1 = ((f32[8,32,2,128]{3,2,1,0:T(2,128)}), f32[8,32,2,128]{3,2,1,0:T(2,128)S(1)}, u32[]{:S(2)}, u32[]{:S(2)}) async-start(f32[8,32,2,128]{3,2,1,0:T(2,128)} %bitcast.22), calls=%async_computation.1 | async-start | bytes 524288 | tf_op jit(solution)/shard_map/all_to_all | solution.py:95
  538.5 5.2 all-to-all-done.1
  543.8 8.7 %scatter_fusion.1 = f32[256,2,128]{2,1,0:T(2,128)S(1)} fusion(f32[256,2,128]{2,1,0:T(2,128)S(1)} %broadcast.154, s32[256]{0:T(256)S(1)} %bitcast.87, f32[256,2,128]{2,1,0:T(2,128)S(1)} %bitcast.82), kind=kCustom, calls=%fused_computation.2 | custom fusion | flops 65536 | bytes 787456 | tf_op jit(solution)/shard_map/scatter-add | solution.py:104
  552.8 3.4 collective-permute-start.1
  558.1 3.6 collective-permute-done.2
  562.3 1.9 collective-permute-start.3
  564.2 2.4 collective-permute-start.4
  566.6 3.2 collective-permute-done.4
  (172 shorter events, 79.3 us)
Async XLA Ops:
  6.5 84.1 %copy-start = (f32[16384]{0:T(1024)S(1)}, f32[16384]{0:T(1024)}, u32[]{:S(2)}) copy-start(f32[16384]{0:T(1024)} %param.12) | copy-start | bytes 196612
  6.5 80.4 %all-gather.4.cloned.1.call-start = ((), (), s32[]{:S(2)}) async-start(), calls=%async_computation.2 | async-start | bytes 4325376 | tf_op jit(solution)/shard_map/all_gather | solution.py:56
  12.4 482.3 %all-to-all-start = ((s32[8,1,32]{2,1,0:T(1,128)}), s32[8,1,32]{2,1,0:T(1,128)S(1)}, u32[]{:S(2)}, u32[]{:S(2)}) async-start(s32[8,1,32]{2,1,0:T(1,128)} %all_to_all.9), calls=%async_computation | async-start | bytes 8192 | tf_op jit(solution)/shard_map/all_to_all | solution.py:98
  92.6 10.4 %collective-permute-start = (f32[4,16384]{1,0:T(4,128)S(1)}, f32[4,16384]{1,0:T(4,128)S(1)}, u32[]{:S(2)}, u32[]{:S(2)}) collective-permute-start(f32[4,16384]{1,0:T(4,128)S(1)} %pad_maximum_fusion.6), channel_id=1, source_target_pairs={{8,0},{16,8},{24,16},{32,24},{40,32},{48,40},{56,48},{64,56},{72,6... | collective-permute-start | bytes 786440 | tf_op jit(solution)/shard_map/while/body/eval_jaxpr/ppermute | solution.py:13
  104.5 10.4 %collective-permute-start = (f32[4,16384]{1,0:T(4,128)S(1)}, f32[4,16384]{1,0:T(4,128)S(1)}, u32[]{:S(2)}, u32[]{:S(2)}) collective-permute-start(f32[4,16384]{1,0:T(4,128)S(1)} %pad_maximum_fusion.6), channel_id=1, source_target_pairs={{8,0},{16,8},{24,16},{32,24},{40,32},{48,40},{56,48},{64,56},{72,6... | collective-permute-start | bytes 786440 | tf_op jit(solution)/shard_map/while/body/eval_jaxpr/ppermute | solution.py:13
  116.3 10.4 %collective-permute-start = (f32[4,16384]{1,0:T(4,128)S(1)}, f32[4,16384]{1,0:T(4,128)S(1)}, u32[]{:S(2)}, u32[]{:S(2)}) collective-permute-start(f32[4,16384]{1,0:T(4,128)S(1)} %pad_maximum_fusion.6), channel_id=1, source_target_pairs={{8,0},{16,8},{24,16},{32,24},{40,32},{48,40},{56,48},{64,56},{72,6... | collective-permute-start | bytes 786440 | tf_op jit(solution)/shard_map/while/body/eval_jaxpr/ppermute | solution.py:13
  128.2 10.4 %collective-permute-start = (f32[4,16384]{1,0:T(4,128)S(1)}, f32[4,16384]{1,0:T(4,128)S(1)}, u32[]{:S(2)}, u32[]{:S(2)}) collective-permute-start(f32[4,16384]{1,0:T(4,128)S(1)} %pad_maximum_fusion.6), channel_id=1, source_target_pairs={{8,0},{16,8},{24,16},{32,24},{40,32},{48,40},{56,48},{64,56},{72,6... | collective-permute-start | bytes 786440 | tf_op jit(solution)/shard_map/while/body/eval_jaxpr/ppermute | solution.py:13
  140.1 10.4 %collective-permute-start = (f32[4,16384]{1,0:T(4,128)S(1)}, f32[4,16384]{1,0:T(4,128)S(1)}, u32[]{:S(2)}, u32[]{:S(2)}) collective-permute-start(f32[4,16384]{1,0:T(4,128)S(1)} %pad_maximum_fusion.6), channel_id=1, source_target_pairs={{8,0},{16,8},{24,16},{32,24},{40,32},{48,40},{56,48},{64,56},{72,6... | collective-permute-start | bytes 786440 | tf_op jit(solution)/shard_map/while/body/eval_jaxpr/ppermute | solution.py:13
  151.9 11.1 %collective-permute-start = (f32[4,16384]{1,0:T(4,128)S(1)}, f32[4,16384]{1,0:T(4,128)S(1)}, u32[]{:S(2)}, u32[]{:S(2)}) collective-permute-start(f32[4,16384]{1,0:T(4,128)S(1)} %pad_maximum_fusion.6), channel_id=1, source_target_pairs={{8,0},{16,8},{24,16},{32,24},{40,32},{48,40},{56,48},{64,56},{72,6... | collective-permute-start | bytes 786440 | tf_op jit(solution)/shard_map/while/body/eval_jaxpr/ppermute | solution.py:13
  164.4 12.2 %collective-permute-start = (f32[4,16384]{1,0:T(4,128)S(1)}, f32[4,16384]{1,0:T(4,128)S(1)}, u32[]{:S(2)}, u32[]{:S(2)}) collective-permute-start(f32[4,16384]{1,0:T(4,128)S(1)} %pad_maximum_fusion.6), channel_id=1, source_target_pairs={{8,0},{16,8},{24,16},{32,24},{40,32},{48,40},{56,48},{64,56},{72,6... | collective-permute-start | bytes 786440 | tf_op jit(solution)/shard_map/while/body/eval_jaxpr/ppermute | solution.py:13
  178.0 13.4 %collective-permute-start = (f32[4,16384]{1,0:T(4,128)S(1)}, f32[4,16384]{1,0:T(4,128)S(1)}, u32[]{:S(2)}, u32[]{:S(2)}) collective-permute-start(f32[4,16384]{1,0:T(4,128)S(1)} %pad_maximum_fusion.6), channel_id=1, source_target_pairs={{8,0},{16,8},{24,16},{32,24},{40,32},{48,40},{56,48},{64,56},{72,6... | collective-permute-start | bytes 786440 | tf_op jit(solution)/shard_map/while/body/eval_jaxpr/ppermute | solution.py:13
  192.9 12.6 %collective-permute-start = (f32[4,16384]{1,0:T(4,128)S(1)}, f32[4,16384]{1,0:T(4,128)S(1)}, u32[]{:S(2)}, u32[]{:S(2)}) collective-permute-start(f32[4,16384]{1,0:T(4,128)S(1)} %pad_maximum_fusion.6), channel_id=1, source_target_pairs={{8,0},{16,8},{24,16},{32,24},{40,32},{48,40},{56,48},{64,56},{72,6... | collective-permute-start | bytes 786440 | tf_op jit(solution)/shard_map/while/body/eval_jaxpr/ppermute | solution.py:13
  206.9 11.7 %collective-permute-start = (f32[4,16384]{1,0:T(4,128)S(1)}, f32[4,16384]{1,0:T(4,128)S(1)}, u32[]{:S(2)}, u32[]{:S(2)}) collective-permute-start(f32[4,16384]{1,0:T(4,128)S(1)} %pad_maximum_fusion.6), channel_id=1, source_target_pairs={{8,0},{16,8},{24,16},{32,24},{40,32},{48,40},{56,48},{64,56},{72,6... | collective-permute-start | bytes 786440 | tf_op jit(solution)/shard_map/while/body/eval_jaxpr/ppermute | solution.py:13
  220.0 10.9 %collective-permute-start = (f32[4,16384]{1,0:T(4,128)S(1)}, f32[4,16384]{1,0:T(4,128)S(1)}, u32[]{:S(2)}, u32[]{:S(2)}) collective-permute-start(f32[4,16384]{1,0:T(4,128)S(1)} %pad_maximum_fusion.6), channel_id=1, source_target_pairs={{8,0},{16,8},{24,16},{32,24},{40,32},{48,40},{56,48},{64,56},{72,6... | collective-permute-start | bytes 786440 | tf_op jit(solution)/shard_map/while/body/eval_jaxpr/ppermute | solution.py:13
  232.3 10.4 %collective-permute-start = (f32[4,16384]{1,0:T(4,128)S(1)}, f32[4,16384]{1,0:T(4,128)S(1)}, u32[]{:S(2)}, u32[]{:S(2)}) collective-permute-start(f32[4,16384]{1,0:T(4,128)S(1)} %pad_maximum_fusion.6), channel_id=1, source_target_pairs={{8,0},{16,8},{24,16},{32,24},{40,32},{48,40},{56,48},{64,56},{72,6... | collective-permute-start | bytes 786440 | tf_op jit(solution)/shard_map/while/body/eval_jaxpr/ppermute | solution.py:13
  244.2 10.4 %collective-permute-start = (f32[4,16384]{1,0:T(4,128)S(1)}, f32[4,16384]{1,0:T(4,128)S(1)}, u32[]{:S(2)}, u32[]{:S(2)}) collective-permute-start(f32[4,16384]{1,0:T(4,128)S(1)} %pad_maximum_fusion.6), channel_id=1, source_target_pairs={{8,0},{16,8},{24,16},{32,24},{40,32},{48,40},{56,48},{64,56},{72,6... | collective-permute-start | bytes 786440 | tf_op jit(solution)/shard_map/while/body/eval_jaxpr/ppermute | solution.py:13
  256.0 10.4 %collective-permute-start = (f32[4,16384]{1,0:T(4,128)S(1)}, f32[4,16384]{1,0:T(4,128)S(1)}, u32[]{:S(2)}, u32[]{:S(2)}) collective-permute-start(f32[4,16384]{1,0:T(4,128)S(1)} %pad_maximum_fusion.6), channel_id=1, source_target_pairs={{8,0},{16,8},{24,16},{32,24},{40,32},{48,40},{56,48},{64,56},{72,6... | collective-permute-start | bytes 786440 | tf_op jit(solution)/shard_map/while/body/eval_jaxpr/ppermute | solution.py:13
  267.9 10.4 %collective-permute-start = (f32[4,16384]{1,0:T(4,128)S(1)}, f32[4,16384]{1,0:T(4,128)S(1)}, u32[]{:S(2)}, u32[]{:S(2)}) collective-permute-start(f32[4,16384]{1,0:T(4,128)S(1)} %pad_maximum_fusion.6), channel_id=1, source_target_pairs={{8,0},{16,8},{24,16},{32,24},{40,32},{48,40},{56,48},{64,56},{72,6... | collective-permute-start | bytes 786440 | tf_op jit(solution)/shard_map/while/body/eval_jaxpr/ppermute | solution.py:13
  279.8 10.4 %collective-permute-start = (f32[4,16384]{1,0:T(4,128)S(1)}, f32[4,16384]{1,0:T(4,128)S(1)}, u32[]{:S(2)}, u32[]{:S(2)}) collective-permute-start(f32[4,16384]{1,0:T(4,128)S(1)} %pad_maximum_fusion.6), channel_id=1, source_target_pairs={{8,0},{16,8},{24,16},{32,24},{40,32},{48,40},{56,48},{64,56},{72,6... | collective-permute-start | bytes 786440 | tf_op jit(solution)/shard_map/while/body/eval_jaxpr/ppermute | solution.py:13
  291.6 10.4 %collective-permute-start = (f32[4,16384]{1,0:T(4,128)S(1)}, f32[4,16384]{1,0:T(4,128)S(1)}, u32[]{:S(2)}, u32[]{:S(2)}) collective-permute-start(f32[4,16384]{1,0:T(4,128)S(1)} %pad_maximum_fusion.6), channel_id=1, source_target_pairs={{8,0},{16,8},{24,16},{32,24},{40,32},{48,40},{56,48},{64,56},{72,6... | collective-permute-start | bytes 786440 | tf_op jit(solution)/shard_map/while/body/eval_jaxpr/ppermute | solution.py:13
  303.5 10.7 %collective-permute-start = (f32[4,16384]{1,0:T(4,128)S(1)}, f32[4,16384]{1,0:T(4,128)S(1)}, u32[]{:S(2)}, u32[]{:S(2)}) collective-permute-start(f32[4,16384]{1,0:T(4,128)S(1)} %pad_maximum_fusion.6), channel_id=1, source_target_pairs={{8,0},{16,8},{24,16},{32,24},{40,32},{48,40},{56,48},{64,56},{72,6... | collective-permute-start | bytes 786440 | tf_op jit(solution)/shard_map/while/body/eval_jaxpr/ppermute | solution.py:13
  315.6 11.8 %collective-permute-start = (f32[4,16384]{1,0:T(4,128)S(1)}, f32[4,16384]{1,0:T(4,128)S(1)}, u32[]{:S(2)}, u32[]{:S(2)}) collective-permute-start(f32[4,16384]{1,0:T(4,128)S(1)} %pad_maximum_fusion.6), channel_id=1, source_target_pairs={{8,0},{16,8},{24,16},{32,24},{40,32},{48,40},{56,48},{64,56},{72,6... | collective-permute-start | bytes 786440 | tf_op jit(solution)/shard_map/while/body/eval_jaxpr/ppermute | solution.py:13
  328.8 13.0 %collective-permute-start = (f32[4,16384]{1,0:T(4,128)S(1)}, f32[4,16384]{1,0:T(4,128)S(1)}, u32[]{:S(2)}, u32[]{:S(2)}) collective-permute-start(f32[4,16384]{1,0:T(4,128)S(1)} %pad_maximum_fusion.6), channel_id=1, source_target_pairs={{8,0},{16,8},{24,16},{32,24},{40,32},{48,40},{56,48},{64,56},{72,6... | collective-permute-start | bytes 786440 | tf_op jit(solution)/shard_map/while/body/eval_jaxpr/ppermute | solution.py:13
  343.2 12.7 %collective-permute-start = (f32[4,16384]{1,0:T(4,128)S(1)}, f32[4,16384]{1,0:T(4,128)S(1)}, u32[]{:S(2)}, u32[]{:S(2)}) collective-permute-start(f32[4,16384]{1,0:T(4,128)S(1)} %pad_maximum_fusion.6), channel_id=1, source_target_pairs={{8,0},{16,8},{24,16},{32,24},{40,32},{48,40},{56,48},{64,56},{72,6... | collective-permute-start | bytes 786440 | tf_op jit(solution)/shard_map/while/body/eval_jaxpr/ppermute | solution.py:13
  357.3 11.8 %collective-permute-start = (f32[4,16384]{1,0:T(4,128)S(1)}, f32[4,16384]{1,0:T(4,128)S(1)}, u32[]{:S(2)}, u32[]{:S(2)}) collective-permute-start(f32[4,16384]{1,0:T(4,128)S(1)} %pad_maximum_fusion.6), channel_id=1, source_target_pairs={{8,0},{16,8},{24,16},{32,24},{40,32},{48,40},{56,48},{64,56},{72,6... | collective-permute-start | bytes 786440 | tf_op jit(solution)/shard_map/while/body/eval_jaxpr/ppermute | solution.py:13
  370.6 11.0 %collective-permute-start = (f32[4,16384]{1,0:T(4,128)S(1)}, f32[4,16384]{1,0:T(4,128)S(1)}, u32[]{:S(2)}, u32[]{:S(2)}) collective-permute-start(f32[4,16384]{1,0:T(4,128)S(1)} %pad_maximum_fusion.6), channel_id=1, source_target_pairs={{8,0},{16,8},{24,16},{32,24},{40,32},{48,40},{56,48},{64,56},{72,6... | collective-permute-start | bytes 786440 | tf_op jit(solution)/shard_map/while/body/eval_jaxpr/ppermute | solution.py:13
  383.0 10.4 %collective-permute-start = (f32[4,16384]{1,0:T(4,128)S(1)}, f32[4,16384]{1,0:T(4,128)S(1)}, u32[]{:S(2)}, u32[]{:S(2)}) collective-permute-start(f32[4,16384]{1,0:T(4,128)S(1)} %pad_maximum_fusion.6), channel_id=1, source_target_pairs={{8,0},{16,8},{24,16},{32,24},{40,32},{48,40},{56,48},{64,56},{72,6... | collective-permute-start | bytes 786440 | tf_op jit(solution)/shard_map/while/body/eval_jaxpr/ppermute | solution.py:13
  394.8 10.4 %collective-permute-start = (f32[4,16384]{1,0:T(4,128)S(1)}, f32[4,16384]{1,0:T(4,128)S(1)}, u32[]{:S(2)}, u32[]{:S(2)}) collective-permute-start(f32[4,16384]{1,0:T(4,128)S(1)} %pad_maximum_fusion.6), channel_id=1, source_target_pairs={{8,0},{16,8},{24,16},{32,24},{40,32},{48,40},{56,48},{64,56},{72,6... | collective-permute-start | bytes 786440 | tf_op jit(solution)/shard_map/while/body/eval_jaxpr/ppermute | solution.py:13
  406.7 10.4 %collective-permute-start = (f32[4,16384]{1,0:T(4,128)S(1)}, f32[4,16384]{1,0:T(4,128)S(1)}, u32[]{:S(2)}, u32[]{:S(2)}) collective-permute-start(f32[4,16384]{1,0:T(4,128)S(1)} %pad_maximum_fusion.6), channel_id=1, source_target_pairs={{8,0},{16,8},{24,16},{32,24},{40,32},{48,40},{56,48},{64,56},{72,6... | collective-permute-start | bytes 786440 | tf_op jit(solution)/shard_map/while/body/eval_jaxpr/ppermute | solution.py:13
  418.5 10.4 %collective-permute-start = (f32[4,16384]{1,0:T(4,128)S(1)}, f32[4,16384]{1,0:T(4,128)S(1)}, u32[]{:S(2)}, u32[]{:S(2)}) collective-permute-start(f32[4,16384]{1,0:T(4,128)S(1)} %pad_maximum_fusion.6), channel_id=1, source_target_pairs={{8,0},{16,8},{24,16},{32,24},{40,32},{48,40},{56,48},{64,56},{72,6... | collective-permute-start | bytes 786440 | tf_op jit(solution)/shard_map/while/body/eval_jaxpr/ppermute | solution.py:13
  430.4 10.4 %collective-permute-start = (f32[4,16384]{1,0:T(4,128)S(1)}, f32[4,16384]{1,0:T(4,128)S(1)}, u32[]{:S(2)}, u32[]{:S(2)}) collective-permute-start(f32[4,16384]{1,0:T(4,128)S(1)} %pad_maximum_fusion.6), channel_id=1, source_target_pairs={{8,0},{16,8},{24,16},{32,24},{40,32},{48,40},{56,48},{64,56},{72,6... | collective-permute-start | bytes 786440 | tf_op jit(solution)/shard_map/while/body/eval_jaxpr/ppermute | solution.py:13
  442.3 10.4 %collective-permute-start = (f32[4,16384]{1,0:T(4,128)S(1)}, f32[4,16384]{1,0:T(4,128)S(1)}, u32[]{:S(2)}, u32[]{:S(2)}) collective-permute-start(f32[4,16384]{1,0:T(4,128)S(1)} %pad_maximum_fusion.6), channel_id=1, source_target_pairs={{8,0},{16,8},{24,16},{32,24},{40,32},{48,40},{56,48},{64,56},{72,6... | collective-permute-start | bytes 786440 | tf_op jit(solution)/shard_map/while/body/eval_jaxpr/ppermute | solution.py:13
  454.1 10.6 %collective-permute-start = (f32[4,16384]{1,0:T(4,128)S(1)}, f32[4,16384]{1,0:T(4,128)S(1)}, u32[]{:S(2)}, u32[]{:S(2)}) collective-permute-start(f32[4,16384]{1,0:T(4,128)S(1)} %pad_maximum_fusion.6), channel_id=1, source_target_pairs={{8,0},{16,8},{24,16},{32,24},{40,32},{48,40},{56,48},{64,56},{72,6... | collective-permute-start | bytes 786440 | tf_op jit(solution)/shard_map/while/body/eval_jaxpr/ppermute | solution.py:13
  466.1 11.7 %collective-permute-start = (f32[4,16384]{1,0:T(4,128)S(1)}, f32[4,16384]{1,0:T(4,128)S(1)}, u32[]{:S(2)}, u32[]{:S(2)}) collective-permute-start(f32[4,16384]{1,0:T(4,128)S(1)} %pad_maximum_fusion.6), channel_id=1, source_target_pairs={{8,0},{16,8},{24,16},{32,24},{40,32},{48,40},{56,48},{64,56},{72,6... | collective-permute-start | bytes 786440 | tf_op jit(solution)/shard_map/while/body/eval_jaxpr/ppermute | solution.py:13
  494.8 49.0 %all-to-all-start.1 = ((f32[8,32,2,128]{3,2,1,0:T(2,128)}), f32[8,32,2,128]{3,2,1,0:T(2,128)S(1)}, u32[]{:S(2)}, u32[]{:S(2)}) async-start(f32[8,32,2,128]{3,2,1,0:T(2,128)} %bitcast.22), calls=%async_computation.1 | async-start | bytes 524288 | tf_op jit(solution)/shard_map/all_to_all | solution.py:95
  552.8 5.3 collective-permute-start.1
  556.2 5.6 collective-permute-start.2
  562.3 4.3 collective-permute-start.3
  564.2 5.6 collective-permute-start.4
Sparse Core Ops, SparseCore 0:
  9.9 76.9 all-gather.3
